TPU v7x, 32 devices: a whole 2x2x4 slice. The times are simulated.
32 devices in a mesh: ctx: 4 (over y, x), head: 8 (over z, core).
Axes of the slice: x: 2, y: 2, z: 4, core: 2. Of those that a mesh axis runs over, the one named last changes fastest.
Arguments:
- hidden_rows: float32 [512, 2304], P(('ctx', 'head')), may hold values from -60 to 60
- segment_ids: int32 [512], replicated, may hold values from 0 to 1, never falling along the last dimension, each value on 1 to 480 neighbouring positions
- w_query: float32 [2304, 6144], P(None, 'head'), may hold values from -0.125 to 0.125
- w_down: float32 [2304, 576], replicated, may hold values from -0.125 to 0.125
- w_up: float32 [512, 8192], P(None, 'head'), may hold values from -0.25 to 0.25
- w_out: float32 [4096, 2304], P('head'), may hold values from -0.09375 to 0.09375
Outputs:
- attended: float32 [512, 2304], P(('ctx', 'head'))
- log_norm: float32 [32, 512], P('head', 'ctx')
All inputs are finite; a program needn't handle non-finite values.
Results may differ from a plain program's by a relative error of at most 0.00015.
Values sent between devices are 32-bit elements; how exact they have to be, the bound alone decides.
No kernel may reach another device: no remote copies, remote signals or barrier semaphores. Data moves between devices by JAX's collectives and lax.ppermute only.
A program may use at most 64 MiB of HBM per device.

v0:
```python
import math

import jax
import jax.numpy as jnp
from jax import lax
from jax.sharding import PartitionSpec as P

KV_RANK = 512
NOPE = 128
ROPE = 64
VDIM = 128


eps_norm = 1e-06
neg_fill = -1e30
precise = lax.Precision.HIGHEST


def from_behind(value, axis, steps):
    count = lax.axis_size(axis)
    first, last = (max(0, -steps), min(count, count - steps))
    return lax.ppermute(value, axis, [(source, source + steps) for source in range(first, last)])


def product(left, right):
    return jnp.dot(left, right, precision=precise, preferred_element_type=jnp.float32)


def normalize(raw_latent):
    compressed = raw_latent[:, :KV_RANK]
    mean_square = jnp.mean(compressed * compressed, axis=1, keepdims=True)
    return jnp.concatenate(
        [compressed * lax.rsqrt(mean_square + eps_norm), raw_latent[:, KV_RANK:]], axis=1
    )


def body(hidden_rows, segment_ids, w_query, w_down, w_up, w_out):
    ctx_count = lax.axis_size("ctx")
    ctx_at = lax.axis_index("ctx")
    head_count = w_query.shape[1] // (NOPE + ROPE)
    queries = product(lax.all_gather(hidden_rows, "head", axis=0, tiled=True), w_query)
    latent = lax.all_gather(normalize(product(hidden_rows, w_down)), "head", axis=0, tiled=True)
    row_count = queries.shape[0]
    queries = queries.reshape(row_count, head_count, NOPE + ROPE).transpose(1, 0, 2)
    score_factor = 1.0 / math.sqrt(NOPE + ROPE)
    offsets = jnp.arange(row_count, dtype=jnp.int32)

    def attend(carry_state, query_heads, query_ctx, block, key_ctx):
        key_start = jnp.maximum(key_ctx, 0)
        query_pos = query_ctx * row_count + offsets
        key_pos = key_start * row_count + offsets
        query_seg = lax.dynamic_slice_in_dim(segment_ids, query_ctx * row_count, row_count)
        key_seg = lax.dynamic_slice_in_dim(segment_ids, key_start * row_count, row_count)
        allowed = (
            (key_pos[None, :] <= query_pos[:, None])
            & (key_seg[None, :] == query_seg[:, None])
            & (key_ctx >= 0)
        )
        up_proj = product(block[:, :KV_RANK], w_up).reshape(row_count, head_count, NOPE + VDIM)
        scores = jnp.einsum(
            "hqd,khd->hqk", query_heads[..., :NOPE], up_proj[..., :NOPE], precision=precise
        )
        scores = scores + jnp.einsum(
            "hqd,kd->hqk", query_heads[..., NOPE:], block[:, KV_RANK:], precision=precise
        )
        scores = jnp.where(allowed[None], scores * score_factor, neg_fill)
        peak_old, total_old, accum_old = carry_state
        peak_new = jnp.maximum(peak_old, jnp.max(scores, axis=2))
        weights = jnp.where(allowed[None], jnp.exp(scores - peak_new[..., None]), 0.0)
        factor = jnp.exp(peak_old - peak_new)
        total_new = total_old * factor + jnp.sum(weights, axis=2)
        accum_new = accum_old * factor[..., None] + jnp.einsum(
            "hqk,khd->hqd", weights, up_proj[..., NOPE:], precision=precise
        )
        return (peak_new, total_new, accum_new)

    start_state = (
        jnp.full((head_count, row_count), neg_fill, jnp.float32),
        jnp.zeros((head_count, row_count), jnp.float32),
        jnp.zeros((head_count, row_count, VDIM), jnp.float32),
    )
    carry_state = attend(start_state, queries, ctx_at, latent, ctx_at)
    moving = latent
    for hop_index in range(1, ctx_count):
        moving = from_behind(moving, "ctx", 1)
        key_ctx = ctx_at - hop_index
        carry_state = attend(carry_state, queries, ctx_at, moving, key_ctx)
    peak_final, total_final, accum_final = carry_state
    head_outputs = accum_final / total_final[..., None]
    log_norm = peak_final + jnp.log(total_final)
    flattened = head_outputs.transpose(1, 0, 2).reshape(row_count, head_count * VDIM)
    attended = lax.psum_scatter(product(flattened, w_out), "head", scatter_dimension=0, tiled=True)
    return (attended, log_norm)


def solution(mesh):
    in_specs = (
        P(("ctx", "head"), None),
        P(),
        P(None, "head"),
        P(),
        P(None, "head"),
        P("head", None),
    )
    out_specs = (P(("ctx", "head"), None), P("head", "ctx"))
    return jax.shard_map(body, mesh=mesh, in_specs=in_specs, out_specs=out_specs, check_vma=False)
```

profile of v0, /device:TPU:0, one launch (start us, length us, event | category | flops | bytes accessed | tf_op | source)
XLA Modules:
  0.0 144.9 jit_solution(3803855338569367121)
XLA Ops:
  8.0 6.9 %fusion.85 = f32[16,576]{1,0:T(8,128)S(1)} fusion(f32[16,2304]{1,0:T(8,128)} %param.6, f32[2304,576]{0,1:T(8,128)} %param.9), kind=kOutput, calls=%fused_computation.124 | convolution fusion | flops 254803968 | bytes 5492736 | tf_op jit(solution)/shard_map/dot_general | solution.py:26
  15.1 17.0 %all_gather.7 = f32[128,576]{1,0:T(8,128)S(1)} all-gather(f32[16,576]{1,0:T(8,128)S(1)} %pad_maximum_fusion), channel_id=1, replica_groups=mesh['ctx'=4,'head'=8] {'head'}, dimensions={0}, use_global_device_ids=true | all-gather | bytes 331776 | tf_op jit(solution)/shard_map/all_gather | solution.py:42
  32.2 4.2 %collective-permute-start = (f32[128,576]{1,0:T(8,128)S(1)}, f32[128,576]{1,0:T(8,128)}, u32[]{:S(2)}, u32[]{:S(2)}) collective-permute-start(f32[128,576]{1,0:T(8,128)S(1)} %all_gather.7), channel_id=1, source_target_pairs={{0,8},{8,16},{16,24},{1,9},{9,17},{17,25},{2,10},{10,18},{18,26},{... | collective-permute-start | bytes 884744 | tf_op jit(solution)/shard_map/ppermute | solution.py:22
  36.4 1.3 fusion.22
  38.2 0.9 fusion.78
  39.1 3.9 %collective-permute-done = f32[128,576]{1,0:T(8,128)} collective-permute-done((f32[128,576]{1,0:T(8,128)S(1)}, f32[128,576]{1,0:T(8,128)}, u32[]{:S(2)}, u32[]{:S(2)}) %collective-permute-start) | collective-permute-done | bytes 294944 | tf_op jit(solution)/shard_map/ppermute | solution.py:22
  43.1 5.2 %collective-permute-start.1 = (f32[128,576]{1,0:T(8,128)}, f32[128,576]{1,0:T(8,128)}, u32[]{:S(2)}, u32[]{:S(2)}) collective-permute-start(f32[128,576]{1,0:T(8,128)} %collective-permute-done), channel_id=1, source_target_pairs={{0,8},{8,16},{16,24},{1,9},{9,17},{17,25},{2,10},{10,18},{18,26},{... | collective-permute-start | bytes 884744 | tf_op jit(solution)/shard_map/ppermute | solution.py:22
  48.3 2.2 %fusion.20 = f32[128,1024]{1,0:T(8,128)S(1)} fusion(f32[512,1024]{1,0:T(8,128)S(1)} %copy-done, f32[128,576]{1,0:T(8,128)} %collective-permute-done), kind=kOutput, calls=%fused_computation.28 | convolution fusion | flops 805306368 | bytes 2883584 | tf_op jit(solution)/shard_map/dot_general | solution.py:26
  50.8 0.9 fusion.77
  51.7 2.8 %collective-permute-done.1 = f32[128,576]{1,0:T(8,128)} collective-permute-done((f32[128,576]{1,0:T(8,128)}, f32[128,576]{1,0:T(8,128)}, u32[]{:S(2)}, u32[]{:S(2)}) %collective-permute-start.1) | collective-permute-done | bytes 294944 | tf_op jit(solution)/shard_map/ppermute | solution.py:22
  54.5 5.1 %collective-permute-start.2 = (f32[128,576]{1,0:T(8,128)}, f32[128,576]{1,0:T(8,128)}, u32[]{:S(2)}, u32[]{:S(2)}) collective-permute-start(f32[128,576]{1,0:T(8,128)} %collective-permute-done.1), channel_id=1, source_target_pairs={{0,8},{8,16},{16,24},{1,9},{9,17},{17,25},{2,10},{10,18},{18,26},{... | collective-permute-start | bytes 884744 | tf_op jit(solution)/shard_map/ppermute | solution.py:22
  59.6 2.2 %fusion.18 = f32[128,1024]{1,0:T(8,128)S(1)} fusion(f32[512,1024]{1,0:T(8,128)S(1)} %copy-done, f32[128,576]{1,0:T(8,128)} %collective-permute-done.1), kind=kOutput, calls=%fused_computation.26 | convolution fusion | flops 805306368 | bytes 2883584 | tf_op jit(solution)/shard_map/dot_general | solution.py:26
  62.1 0.9 fusion.76
  63.0 1.9 %collective-permute-done.2 = f32[128,576]{1,0:T(8,128)} collective-permute-done((f32[128,576]{1,0:T(8,128)}, f32[128,576]{1,0:T(8,128)}, u32[]{:S(2)}, u32[]{:S(2)}) %collective-permute-start.2) | collective-permute-done | bytes 294944 | tf_op jit(solution)/shard_map/ppermute | solution.py:22
  64.9 2.2 %fusion.16 = f32[128,1024]{1,0:T(8,128)S(1)} fusion(f32[512,1024]{1,0:T(8,128)S(1)} %copy-done, f32[128,576]{1,0:T(8,128)} %collective-permute-done.2), kind=kOutput, calls=%fused_computation.24 | convolution fusion | flops 805306368 | bytes 2883584 | tf_op jit(solution)/shard_map/dot_general | solution.py:26
  68.3 13.9 %fusion.84 = f32[128,768]{0,1:T(8,128)S(1)} fusion(f32[128,2304]{1,0:T(8,128)} %all-gather.2.cloned.1.call-done, f32[2304,768]{1,0:T(8,128)} %param.8), kind=kOutput, calls=%fused_computation.123 | convolution fusion | flops 2717908992 | bytes 8650752 | tf_op jit(solution)/shard_map/dot_general | solution.py:26
  82.4 1.7 %fusion.25 = f32[4,128,128]{1,2,0:T(8,128)S(1)} fusion(f32[128,4,128]{2,1,0:T(4,128)} %get-tuple-element.9, f32[4,128,192]{2,1,0:T(8,128)S(1)} %bitcast.122), kind=kOutput, calls=%fused_computation.33 | convolution fusion | flops 100663296 | bytes 786432 | tf_op jit(solution)/shard_map/hqd,khd->hqk/dot_general | solution.py:60
  84.0 1.6 %fusion.28 = f32[4,128,128]{1,2,0:T(8,128)S(1)} fusion(f32[128,4,128]{2,1,0:T(4,128)} %get-tuple-element.11, f32[4,128,192]{2,1,0:T(8,128)S(1)} %bitcast.123), kind=kOutput, calls=%fused_computation.36 | convolution fusion | flops 100663296 | bytes 786432 | tf_op jit(solution)/shard_map/hqd,khd->hqk/dot_general | solution.py:60
  85.7 1.6 %fusion.31 = f32[4,128,128]{1,2,0:T(8,128)S(1)} fusion(f32[128,4,128]{2,1,0:T(4,128)} %get-tuple-element.13, f32[4,128,192]{2,1,0:T(8,128)S(1)} %bitcast.124), kind=kOutput, calls=%fused_computation.39 | convolution fusion | flops 100663296 | bytes 786432 | tf_op jit(solution)/shard_map/hqd,khd->hqk/dot_general | solution.py:60
  88.4 1.3 fusion.80
  89.7 1.3 fusion.81
  91.1 1.3 fusion.82
  95.1 5.8 %fusion.86 = f32[128,2304]{1,0:T(8,128)} fusion(f32[128,512]{0,1:T(8,128)S(1)} %bitcast.131, f32[512,2304]{1,0:T(8,128)} %param.11), kind=kOutput, calls=%fused_computation.125 | convolution fusion | flops 1811939328 | bytes 6160384 | tf_op jit(solution)/shard_map/dot_general | solution.py:26
  101.6 36.4 %reduce-scatter.2.cloned.1.call-done = f32[16,2304]{1,0:T(8,128)} async-done(((f32[128,2304]{1,0:T(8,128)}), f32[16,2304]{1,0:T(8,128)}) %reduce-scatter.2.cloned.1.call-update) | async-done | bytes 147472 | tf_op jit(solution)/shard_map/reduce_scatter | solution.py:92
  (48 shorter events, 7.8 us)
Async XLA Ops:
  7.2 29.2 %copy-start = (f32[512,1024]{1,0:T(8,128)S(1)}, f32[512,1024]{1,0:T(8,128)}, u32[]{:S(2)}) copy-start(f32[512,1024]{1,0:T(8,128)} %param.10) | copy-start | bytes 6291460
  7.2 61.1 %all-gather.2.cloned.1.call-start = ((), (), s32[]{:S(2)}) async-start(), calls=%async_computation.1 | async-start | bytes 1327104 | tf_op jit(solution)/shard_map/all_gather | solution.py:41
  7.9 130.1 %reduce-scatter.2.cloned.1.call-start = ((), (), s32[]{:S(2)}) async-start(), calls=%async_computation.2 | async-start | bytes 1327104 | tf_op jit(solution)/shard_map/reduce_scatter | solution.py:92
  14.9 22.8 %copy-start.6 = (s32[512]{0:T(512)S(1)}, s32[512]{0:T(512)}, u32[]{:S(2)}) copy-start(s32[512]{0:T(512)} %param.7) | copy-start | bytes 6148
  32.2 10.9 %collective-permute-start = (f32[128,576]{1,0:T(8,128)S(1)}, f32[128,576]{1,0:T(8,128)}, u32[]{:S(2)}, u32[]{:S(2)}) collective-permute-start(f32[128,576]{1,0:T(8,128)S(1)} %all_gather.7), channel_id=1, source_target_pairs={{0,8},{8,16},{16,24},{1,9},{9,17},{17,25},{2,10},{10,18},{18,26},{... | collective-permute-start | bytes 884744 | tf_op jit(solution)/shard_map/ppermute | solution.py:22
  43.1 11.4 %collective-permute-start.1 = (f32[128,576]{1,0:T(8,128)}, f32[128,576]{1,0:T(8,128)}, u32[]{:S(2)}, u32[]{:S(2)}) collective-permute-start(f32[128,576]{1,0:T(8,128)} %collective-permute-done), channel_id=1, source_target_pairs={{0,8},{8,16},{16,24},{1,9},{9,17},{17,25},{2,10},{10,18},{18,26},{... | collective-permute-start | bytes 884744 | tf_op jit(solution)/shard_map/ppermute | solution.py:22
  54.5 10.4 %collective-permute-start.2 = (f32[128,576]{1,0:T(8,128)}, f32[128,576]{1,0:T(8,128)}, u32[]{:S(2)}, u32[]{:S(2)}) collective-permute-start(f32[128,576]{1,0:T(8,128)} %collective-permute-done.1), channel_id=1, source_target_pairs={{0,8},{8,16},{16,24},{1,9},{9,17},{17,25},{2,10},{10,18},{18,26},{... | collective-permute-start | bytes 884744 | tf_op jit(solution)/shard_map/ppermute | solution.py:22
  82.4 4.9 %copy-start.2 = (f32[128,4,128]{2,1,0:T(4,128)S(1)}, f32[128,4,128]{2,1,0:T(4,128)}, u32[]{:S(2)}) copy-start(f32[128,4,128]{2,1,0:T(4,128)} %get-tuple-element.14) | copy-start | bytes 786436
  88.4 4.3 %copy-start.1 = (f32[128,4,128]{2,1,0:T(4,128)S(1)}, f32[128,4,128]{2,1,0:T(4,128)}, u32[]{:S(2)}) copy-start(f32[128,4,128]{2,1,0:T(4,128)} %get-tuple-element.15) | copy-start | bytes 786436
  89.7 3.6 %copy-start.3 = (f32[128,4,128]{2,1,0:T(4,128)S(1)}, f32[128,4,128]{2,1,0:T(4,128)}, u32[]{:S(2)}) copy-start(f32[128,4,128]{2,1,0:T(4,128)} %get-tuple-element.12) | copy-start | bytes 786436
  91.1 2.9 %copy-start.4 = (f32[128,4,128]{2,1,0:T(4,128)S(1)}, f32[128,4,128]{2,1,0:T(4,128)}, u32[]{:S(2)}) copy-start(f32[128,4,128]{2,1,0:T(4,128)} %get-tuple-element.10) | copy-start | bytes 786436
  92.4 2.1 %copy-start.5 = (f32[128,4,128]{2,1,0:T(4,128)S(1)}, f32[128,4,128]{2,1,0:T(4,128)}, u32[]{:S(2)}) copy-start(f32[128,4,128]{2,1,0:T(4,128)} %get-tuple-element.8) | copy-start | bytes 786436
Sparse Core Ops, SparseCore 0:
  9.6 27.4 all-gather.1
  101.1 36.8 reduce-scatter.1
where the time goes:
time: 145 us
  matrix products  46.9 us (32%)
  waiting for transfers between devices  45.8 us (32%)
  blocking collectives  17 us (12%)
  starting transfers between devices  14.6 us (10%)
  between operations  14.4 us (10%)
  local copies, waits for them, and re-layouts  4.89 us (3%)
    reduce_scatter x1, waiting for transfers between devices, body(): lax.psum_scatter(product(flattened, w_out), 'head', scatter_dimension=0,...  36.4 us
    dot_general x7, matrix products, product(): jnp.dot(left, right, precision=precise, preferred_element_type=jnp.float32)  34.6 us
    all_gather x1, blocking collectives, body(): lax.all_gather(normalize(product(hidden_rows, w_down)), 'head', axis=0, t...  17 us
    ppermute x3, starting transfers between devices, from_behind(): lax.ppermute(value, axis, [(source, source + steps) for source in range(f...  14.5 us
    ppermute x3, waiting for transfers between devices, from_behind(): lax.ppermute(value, axis, [(source, source + steps) for source in range(f...  8.65 us
    dot_general x4, matrix products, attend(): jnp.einsum('hqd,khd->hqk', query_heads[..., :NOPE], up_proj[..., :NOPE],...  5.53 us
    dot_general x4, matrix products, attend(): jnp.einsum('hqd,kd->hqk', query_heads[..., NOPE:], block[:, KV_RANK:], pr...  4.41 us
  transfers between devices with their start and end apart: 5, of which 4 were waited for; matrix products, arithmetic and copies ran while one was open for 14% of the time, Pallas kernels for 0%

commit v1 on v0

v1 whole, which is shorter than its diff:
```python
import math

import jax
import jax.numpy as jnp
from jax import lax
from jax.sharding import PartitionSpec as P

KV_RANK = 512
NOPE = 128
ROPE = 64
VDIM = 128

eps_norm = 1e-06
neg_fill = -1e30
precise = lax.Precision.HIGH


def product(left, right):
    return jnp.dot(left, right, precision=precise, preferred_element_type=jnp.float32)


def partner_swap(value):
    count = lax.axis_size("head")
    return lax.ppermute(value, "head", [(i, i ^ 1) for i in range(count)])


def chip_shift(value, step):
    count = lax.axis_size("head")
    return lax.ppermute(value, "head", [(i, (i + 2 * step) % count) for i in range(count)])


def gather_head(block):
    count = lax.axis_size("head")
    chips = count // 2
    me = lax.axis_index("head")
    chip, core = me // 2, me % 2
    mine = jnp.stack([block] + [chip_shift(block, s) for s in range(1, chips)])
    theirs = partner_swap(mine)
    first = jnp.where(core == 0, mine, theirs)
    second = jnp.where(core == 0, theirs, mine)
    both = jnp.concatenate([first, second], axis=1)
    order = (chip - jnp.arange(chips)) % chips
    both = jnp.take(both, order, axis=0)
    return both.reshape(-1, block.shape[1])


def scatter_head(partial):
    count = lax.axis_size("head")
    chips = count // 2
    rows = partial.shape[0] // count
    me = lax.axis_index("head")
    chip, core = me // 2, me % 2
    blocks = partial.reshape(chips, 2, rows, partial.shape[1])
    keep = lax.dynamic_index_in_dim(blocks, core, 1, keepdims=False)
    give = lax.dynamic_index_in_dim(blocks, 1 - core, 1, keepdims=False)
    pair = keep + partner_swap(give)
    total = lax.dynamic_index_in_dim(pair, chip, 0, keepdims=False)
    for s in range(1, chips):
        out = lax.dynamic_index_in_dim(pair, (chip + s) % chips, 0, keepdims=False)
        total = total + chip_shift(out, s)
    return total


def body(hidden_rows, segment_ids, w_query, w_down, w_up, w_out):
    ctx_count = lax.axis_size("ctx")
    ctx_at = lax.axis_index("ctx")
    head_count = w_query.shape[1] // (NOPE + ROPE)
    score_factor = 1.0 / math.sqrt(NOPE + ROPE)
    hidden = gather_head(hidden_rows)
    row_count = hidden.shape[0]
    raw = product(hidden, w_down)
    compressed = raw[:, :KV_RANK]
    mean_square = jnp.mean(compressed * compressed, axis=1, keepdims=True)
    latent = jnp.concatenate([compressed * lax.rsqrt(mean_square + eps_norm), raw[:, KV_RANK:]], axis=1)
    blocks = [latent]
    for step in range(1, ctx_count):
        pairs = [(i, i + step) for i in range(ctx_count - step)]
        blocks.append(lax.ppermute(latent, "ctx", pairs))
    queries = product(hidden, w_query).reshape(row_count, head_count, NOPE + ROPE)
    keys_all = jnp.concatenate(blocks, axis=0)
    offsets = jnp.arange(row_count, dtype=jnp.int32)
    key_pos = jnp.concatenate([(ctx_at - step) * row_count + offsets for step in range(ctx_count)])
    query_pos = ctx_at * row_count + offsets
    key_seg = jnp.take(segment_ids, jnp.maximum(key_pos, 0))
    query_seg = key_seg[:row_count]
    allowed = (
        (key_pos[None, :] <= query_pos[:, None])
        & (key_seg[None, :] == query_seg[:, None])
        & (key_pos >= 0)[None, :]
    )
    up = product(keys_all[:, :KV_RANK], w_up).reshape(-1, head_count, NOPE + VDIM)
    scores = jnp.einsum("qhd,khd->hqk", queries[..., :NOPE], up[..., :NOPE], precision=precise)
    scores = scores + jnp.einsum("qhd,kd->hqk", queries[..., NOPE:], keys_all[:, KV_RANK:], precision=precise)
    scores = jnp.where(allowed[None], scores * score_factor, neg_fill)
    peak = jnp.max(scores, axis=2)
    weights = jnp.where(allowed[None], jnp.exp(scores - peak[..., None]), 0.0)
    total = jnp.sum(weights, axis=2)
    out = jnp.einsum("hqk,khd->qhd", weights, up[..., NOPE:], precision=precise)
    out = out / total.T[..., None]
    log_norm = peak + jnp.log(total)
    partial = product(out.reshape(row_count, head_count * VDIM), w_out)
    return (scatter_head(partial), log_norm)


def solution(mesh):
    in_specs = (
        P(("ctx", "head"), None),
        P(),
        P(None, "head"),
        P(),
        P(None, "head"),
        P("head", None),
    )
    out_specs = (P(("ctx", "head"), None), P("head", "ctx"))
    return jax.shard_map(body, mesh=mesh, in_specs=in_specs, out_specs=out_specs, check_vma=False)
```

time: 145 us -> 88.1 us (0.61)
  matrix products: 46.9 us -> 17.5 us
  waiting for transfers between devices: 45.8 us -> 22.9 us
  blocking collectives: 17 us -> 0 us
  local copies, waits for them, and re-layouts: 4.89 us -> 20.8 us
  between operations: 14.4 us -> 1.04 us
  other arithmetic: 1.32 us -> 6.22 us
  starting transfers between devices: 14.6 us -> 19.2 us
    reduce_scatter x1 -> x0, waiting for transfers between devices: 36.4 us -> none  [body(): lax.psum_scatter(product(flattened, w_out), 'head', scatter_dimension=0,...]
    dot_general x7 -> x4, matrix products: 34.6 us -> 14.9 us  [product(): jnp.dot(left, right, precision=precise, preferred_element_type=jnp.float32)]
    all_gather x1 -> x0, blocking collectives: 17 us -> none  [body(): lax.all_gather(normalize(product(hidden_rows, w_down)), 'head', axis=0, t...]
    ppermute x3 -> x11, waiting for transfers between devices: 8.65 us -> 22.9 us  [the longest x6 12.1 us: chip_shift(): lax.ppermute(value, 'head', [(i, (i + 2 * step) % count) for i in range(c...]
    dot_general x12 -> x3, matrix products: 12.3 us -> 2.64 us  [the longest x1 1.16 us: body(): out = jnp.einsum('hqk,khd->qhd', weights, up[..., NOPE:], precision=precise)]
    unnamed x14 -> x29, local copies, waits for them, and re-layouts: 0.03 us -> 9.22 us
    gather x0 -> x2, local copies, waits for them, and re-layouts: none -> 5.37 us  [the longest x1 3.48 us: body(): key_seg = jnp.take(segment_ids, jnp.maximum(key_pos, 0))]
    ppermute x3 -> x11, starting transfers between devices: 14.5 us -> 19.2 us  [the longest x6 10.8 us: chip_shift(): lax.ppermute(value, 'head', [(i, (i + 2 * step) % count) for i in range(c...]
  transfers between devices with their start and end apart: 5 -> 11, of which waited for: 4 -> 6; matrix products, arithmetic and copies ran while one was open for 14% -> 18% of each run, Pallas kernels for 0% -> 0%
where the time goes in v1:
time: 88.1 us; the launch traced here: 87.6 us
  waiting for transfers between devices  22.9 us (26%)
  local copies, waits for them, and re-layouts  20.8 us (24%)
  starting transfers between devices  19.2 us (22%)
  matrix products  17.5 us (20%)
  other arithmetic  6.22 us (7%)
  between operations  1.04 us (1%)
    dot_general x4, matrix products, product(): jnp.dot(left, right, precision=precise, preferred_element_type=jnp.float32)  14.9 us
    ppermute x6, waiting for transfers between devices, chip_shift(): lax.ppermute(value, 'head', [(i, (i + 2 * step) % count) for i in range(c...  12.1 us
    ppermute x6, starting transfers between devices, chip_shift(): lax.ppermute(value, 'head', [(i, (i + 2 * step) % count) for i in range(c...  10.8 us
    unnamed x29, local copies, waits for them, and re-layouts  9.22 us
    ppermute x3, starting transfers between devices, body(): blocks.append(lax.ppermute(latent, 'ctx', pairs))  8.33 us
    ppermute x3, waiting for transfers between devices, body(): blocks.append(lax.ppermute(latent, 'ctx', pairs))  7.1 us
    ppermute x2, waiting for transfers between devices, partner_swap(): return lax.ppermute(value, 'head', [(i, i ^ 1) for i in range(count)])  3.74 us
    gather x1, local copies, waits for them, and re-layouts, body(): key_seg = jnp.take(segment_ids, jnp.maximum(key_pos, 0))  3.48 us
  transfers between devices with their start and end apart: 11, of which 6 were waited for; matrix products, arithmetic and copies ran while one was open for 18% of the time, Pallas kernels for 0%

profile of v1, /device:TPU:0, one launch (start us, length us, event | category | flops | bytes accessed | tf_op | source)
XLA Modules:
  0.0 87.6 jit_solution(5300934752445249330)
XLA Ops:
  0.6 5.1 %collective-permute-start.2 = (f32[16,2304]{1,0:T(8,128)}, f32[16,2304]{1,0:T(8,128)S(1)}, u32[]{:S(2)}, u32[]{:S(2)}) collective-permute-start(f32[16,2304]{1,0:T(8,128)} %param.6), channel_id=1, source_target_pairs={{0,6},{1,7},{2,0},{3,1},{4,2},{5,3},{6,4},{7,5},{8,14},{9,15},{10,... | collective-permute-start | bytes 442376 | tf_op jit(solution)/shard_map/ppermute | solution.py:29
  5.8 1.0 %collective-permute-start = (f32[16,2304]{1,0:T(8,128)}, f32[16,2304]{1,0:T(8,128)S(1)}, u32[]{:S(2)}, u32[]{:S(2)}) collective-permute-start(f32[16,2304]{1,0:T(8,128)} %param.6), channel_id=1, source_target_pairs={{0,2},{1,3},{2,4},{3,5},{4,6},{5,7},{6,0},{7,1},{8,10},{9,11},{10,... | collective-permute-start | bytes 442376 | tf_op jit(solution)/shard_map/ppermute | solution.py:29
  7.1 8.0 %copy.15 = f32[2304,768]{0,1:T(8,128)} copy(f32[2304,768]{1,0:T(8,128)} %param.8) | data formatting | bytes 14155776 | tf_op args[2]
  15.1 3.5 %gather_fusion.1 = s32[512]{0:T(512)S(1)} fusion(s32[512]{0:T(512)S(1)} %copy-done.1, s32[1024]{0:T(1024)S(1)} %pad_clamp_fusion), kind=kCustom, calls=%fused_computation.1 | custom fusion | bytes 6144 | tf_op jit(solution)/shard_map/jit(_take)/gather | solution.py:84
  20.3 1.4 %collective-permute-done.3 = f32[4,16,2304]{2,1,0:T(8,128)S(1)} collective-permute-done((f32[4,16,2304]{2,1,0:T(8,128)}, f32[4,16,2304]{2,1,0:T(8,128)S(1)}, u32[]{:S(2)}, u32[]{:S(2)}) %collective-permute-start.3) | collective-permute-done | bytes 589856 | tf_op jit(solution)/shard_map/ppermute | solution.py:24
  21.8 1.2 %pad_maximum_fusion = f32[4,32,2304]{2,1,0:T(8,128)} fusion(f32[4,16,2304]{2,1,0:T(8,128)S(1)} %get-tuple-element.7, f32[4,16,2304]{2,1,0:T(8,128)S(1)} %get-tuple-element.6), kind=kLoop, calls=%fused_computation.8 | loop fusion | flops 294912 | bytes 2359296 | tf_op jit(solution)/shard_map/concatenate | solution.py:41
  23.0 1.9 %gather_fusion = f32[4,32,2304]{2,1,0:T(8,128)S(1)} fusion(f32[4,32,2304]{2,1,0:T(8,128)} %pad_maximum_fusion, s32[1024]{0:T(1024)S(1)} %pad_clamp_fusion.1), kind=kCustom, calls=%fused_computation | custom fusion | bytes 2359312 | tf_op jit(solution)/shard_map/jit(_take)/gather | solution.py:43
  25.0 4.9 %fusion.39 = f32[128,576]{0,1:T(8,128)S(1)} fusion(f32[128,2304]{1,0:T(8,128)S(1)} %bitcast_select_fusion, f32[2304,576]{0,1:T(8,128)} %param.9), kind=kOutput, calls=%fused_computation.83 | convolution fusion | flops 1019215872 | bytes 6782976 | tf_op jit(solution)/shard_map/dot_general | solution.py:19
  30.1 4.4 %collective-permute-start.6 = (f32[128,576]{0,1:T(8,128)S(1)}, f32[128,576]{0,1:T(8,128)S(1)}, u32[]{:S(2)}, u32[]{:S(2)}) collective-permute-start(f32[128,576]{0,1:T(8,128)S(1)} %pad_maximum_fusion.3), channel_id=1, source_target_pairs={{0,24},{1,25},{2,26},{3,27},{4,28},{5,29},{6,30},{7,31}} | collective-permute-start | bytes 884744 | tf_op jit(solution)/shard_map/ppermute | solution.py:78
  34.5 1.3 %collective-permute-start.5 = (f32[128,576]{0,1:T(8,128)S(1)}, f32[128,576]{0,1:T(8,128)S(1)}, u32[]{:S(2)}, u32[]{:S(2)}) collective-permute-start(f32[128,576]{0,1:T(8,128)S(1)} %pad_maximum_fusion.3), channel_id=1, source_target_pairs={{0,16},{8,24},{1,17},{9,25},{2,18},{10,26},{3,19},{11,27},{4,20},{... | collective-permute-start | bytes 884744 | tf_op jit(solution)/shard_map/ppermute | solution.py:78
  35.8 2.7 %collective-permute-start.4 = (f32[128,576]{0,1:T(8,128)S(1)}, f32[128,576]{0,1:T(8,128)S(1)}, u32[]{:S(2)}, u32[]{:S(2)}) collective-permute-start(f32[128,576]{0,1:T(8,128)S(1)} %pad_maximum_fusion.3), channel_id=1, source_target_pairs={{0,8},{8,16},{16,24},{1,9},{9,17},{17,25},{2,10},{10,18},{18,26},{... | collective-permute-start | bytes 884744 | tf_op jit(solution)/shard_map/ppermute | solution.py:78
  38.6 2.9 %fusion.40 = f32[128,4,192]{0,2,1:T(8,128)S(1)} fusion(f32[128,2304,1]{1,0,2:T(8,128)S(1)} %bitcast.71, f32[4,192,2304]{2,1,0:T(8,128)S(1)} %bitcast.70), kind=kOutput, calls=%fused_computation.84 | convolution fusion | flops 1358954496 | bytes 8650752 | tf_op jit(solution)/shard_map/dot_general | solution.py:19
  41.9 6.8 %collective-permute-done.5 = f32[128,576]{0,1:T(8,128)S(1)} collective-permute-done((f32[128,576]{0,1:T(8,128)S(1)}, f32[128,576]{0,1:T(8,128)S(1)}, u32[]{:S(2)}, u32[]{:S(2)}) %collective-permute-start.5) | collective-permute-done | bytes 294944 | tf_op jit(solution)/shard_map/ppermute | solution.py:78
  49.5 3.3 %fusion.6 = f32[512,1024]{1,0:T(8,128)} fusion(f32[512,1024]{1,0:T(8,128)S(1)} %copy-done, f32[512,576]{0,1:T(8,128)S(1)} %pad_maximum_fusion.1), kind=kOutput, calls=%fused_computation.13 | convolution fusion | flops 1610612736 | bytes 5242880 | tf_op jit(solution)/shard_map/dot_general | solution.py:19
  52.7 3.1 %reshape.297 = f32[512,4,256]{2,1,0:T(4,128)} reshape(f32[512,1024]{1,0:T(8,128)} %fusion.6) | data formatting | bytes 4194304 | tf_op jit(solution)/shard_map/reshape | solution.py:91
  55.9 1.7 %fusion.37 = (f32[512,4,128]{2,1,0:T(4,128)S(1)}, f32[512,4,128]{2,1,0:T(4,128)S(1)}) fusion(f32[512,4,256]{2,1,0:T(4,128)} %reshape.297), kind=kLoop, calls=%fused_computation.81 | loop fusion | bytes 4194304 | tf_op jit(solution)/shard_map/slice | solution.py:92
  59.9 1.2 %fusion.5 = f32[128,4,128]{0,2,1:T(8,128)S(1)} fusion(f32[512,4,128]{2,1,0:T(4,128)S(1)} %get-tuple-element.5, f32[4,128,512]{2,1,0:T(8,128)S(1)} %get-tuple-element.12, f32[4,128]{1,0:T(4,128)S(1)} %get-tuple-element.11, pred[128,512]{1,0:T(8,128)(4,1)S(1)} %copy-done.9, f32[128,4]{0,1:T(4,128)S(1)} %bitcast.80), kind=kOutput, calls=%fused_computation.12 | convolution fusion | flops 201916416 | bytes 2428928 | tf_op jit(solution)/shard_map/hqk,khd->qhd/dot_general | solution.py:98
  61.3 3.8 %fusion = f32[4,2,16,2304]{3,2,1,0:T(8,128)S(1)} fusion(f32[4,2,16,512]{3,2,1,0:T(8,128)S(1)} %dot_general.35, f32[512,2304]{1,0:T(8,128)} %param.11), kind=kOutput, calls=%fused_computation.2 | convolution fusion | flops 905969664 | bytes 6160384 | tf_op jit(solution)/shard_map/dot_general | solution.py:19
  66.1 2.3 %collective-permute-done.7 = f32[4,16,2304]{2,1,0:T(8,128)} collective-permute-done((f32[4,16,2304]{2,1,0:T(8,128)}, f32[4,16,2304]{2,1,0:T(8,128)}, u32[]{:S(2)}, u32[]{:S(2)}) %collective-permute-start.7) | collective-permute-done | bytes 589856 | tf_op jit(solution)/shard_map/ppermute | solution.py:24
  68.4 1.1 %bitcast_add_fusion = f32[4,16,2304]{2,1,0:T(8,128)S(1)} fusion(f32[4,16,2304]{2,1,0:T(8,128)} %collective-permute-done.7, f32[4,2,16,2304]{3,2,1,0:T(8,128)S(1)} %fusion, s32[]{:T(128)S(6)} %select_n.140), kind=kLoop, calls=%fused_computation.21 | loop fusion | flops 147456 | bytes 1769476 | tf_op jit(solution)/shard_map/add | solution.py:56
  69.6 2.9 %collective-permute-start.10 = (f32[16,2304]{1,0:T(8,128)S(1)}, f32[16,2304]{1,0:T(8,128)S(1)}, u32[]{:S(2)}, u32[]{:S(2)}) collective-permute-start(f32[16,2304]{1,0:T(8,128)S(1)} %get-tuple-element.9), channel_id=1, source_target_pairs={{0,6},{1,7},{2,0},{3,1},{4,2},{5,3},{6,4},{7,5},{8,14},{9,15},{10,... | collective-permute-start | bytes 442376 | tf_op jit(solution)/shard_map/ppermute | solution.py:29
  72.5 1.1 %collective-permute-start.9 = (f32[16,2304]{1,0:T(8,128)S(1)}, f32[16,2304]{1,0:T(8,128)S(1)}, u32[]{:S(2)}, u32[]{:S(2)}) collective-permute-start(f32[16,2304]{1,0:T(8,128)S(1)} %get-tuple-element.10), channel_id=1, source_target_pairs={{0,4},{1,5},{2,6},{3,7},{4,0},{5,1},{6,2},{7,3},{8,12},{9,13},{10,... | collective-permute-start | bytes 442376 | tf_op jit(solution)/shard_map/ppermute | solution.py:29
  74.9 1.9 %collective-permute-done.10 = f32[16,2304]{1,0:T(8,128)S(1)} collective-permute-done((f32[16,2304]{1,0:T(8,128)S(1)}, f32[16,2304]{1,0:T(8,128)S(1)}, u32[]{:S(2)}, u32[]{:S(2)}) %collective-permute-start.10) | collective-permute-done | bytes 147488 | tf_op jit(solution)/shard_map/ppermute | solution.py:29
  76.8 10.1 %collective-permute-done.9 = f32[16,2304]{1,0:T(8,128)S(1)} collective-permute-done((f32[16,2304]{1,0:T(8,128)S(1)}, f32[16,2304]{1,0:T(8,128)S(1)}, u32[]{:S(2)}, u32[]{:S(2)}) %collective-permute-start.9) | collective-permute-done | bytes 147488 | tf_op jit(solution)/shard_map/ppermute | solution.py:29
  (74 shorter events, 9.0 us)
Async XLA Ops:
  0.6 48.9 %copy-start = (f32[512,1024]{1,0:T(8,128)S(1)}, f32[512,1024]{1,0:T(8,128)}, u32[]{:S(2)}) copy-start(f32[512,1024]{1,0:T(8,128)} %param.10) | copy-start | bytes 6291460
  0.6 18.0 %collective-permute-start.2 = (f32[16,2304]{1,0:T(8,128)}, f32[16,2304]{1,0:T(8,128)S(1)}, u32[]{:S(2)}, u32[]{:S(2)}) collective-permute-start(f32[16,2304]{1,0:T(8,128)} %param.6), channel_id=1, source_target_pairs={{0,6},{1,7},{2,0},{3,1},{4,2},{5,3},{6,4},{7,5},{8,14},{9,15},{10,... | collective-permute-start | bytes 442376 | tf_op jit(solution)/shard_map/ppermute | solution.py:29
  5.8 12.8 %collective-permute-start.1 = (f32[16,2304]{1,0:T(8,128)}, f32[16,2304]{1,0:T(8,128)S(1)}, u32[]{:S(2)}, u32[]{:S(2)}) collective-permute-start(f32[16,2304]{1,0:T(8,128)} %param.6), channel_id=1, source_target_pairs={{0,4},{1,5},{2,6},{3,7},{4,0},{5,1},{6,2},{7,3},{8,12},{9,13},{10,... | collective-permute-start | bytes 442376 | tf_op jit(solution)/shard_map/ppermute | solution.py:29
  5.8 12.9 %collective-permute-start = (f32[16,2304]{1,0:T(8,128)}, f32[16,2304]{1,0:T(8,128)S(1)}, u32[]{:S(2)}, u32[]{:S(2)}) collective-permute-start(f32[16,2304]{1,0:T(8,128)} %param.6), channel_id=1, source_target_pairs={{0,2},{1,3},{2,4},{3,5},{4,6},{5,7},{6,0},{7,1},{8,10},{9,11},{10,... | collective-permute-start | bytes 442376 | tf_op jit(solution)/shard_map/ppermute | solution.py:29
  7.1 8.0 %copy-start.1 = (s32[512]{0:T(512)S(1)}, s32[512]{0:T(512)}, u32[]{:S(2)}) copy-start(s32[512]{0:T(512)} %param.7) | copy-start | bytes 6148
  15.1 3.5 %copy-start.8 = (f32[16,2304]{1,0:T(8,128)S(1)}, f32[16,2304]{1,0:T(8,128)}, u32[]{:S(2)}) copy-start(f32[16,2304]{1,0:T(8,128)} %param.6) | copy-start | bytes 442372
  19.5 2.2 %collective-permute-start.3 = (f32[4,16,2304]{2,1,0:T(8,128)}, f32[4,16,2304]{2,1,0:T(8,128)S(1)}, u32[]{:S(2)}, u32[]{:S(2)}) collective-permute-start(f32[4,16,2304]{2,1,0:T(8,128)} %pad_maximum_fusion.2), channel_id=1, source_target_pairs={{0,1},{1,0},{2,3},{3,2},{4,5},{5,4},{6,7},{7,6},{8,9},{9,8},{10,11... | collective-permute-start | bytes 1769480 | tf_op jit(solution)/shard_map/ppermute | solution.py:24
  24.9 13.8 %slice-start = ((s8[7077888]{0:T(1024)(128)(4,1)}), s8[4194304]{0:T(1024)(128)(4,1)S(1)}, s32[]{:S(2)}) async-start(s8[7077888]{0:T(1024)(128)(4,1)} %bitcast.68), calls=%async_computation | async-start | bytes 8388608
  25.0 13.6 %slice-start.1 = ((s8[7077888]{0:T(1024)(128)(4,1)}), s8[2883584]{0:T(1024)(128)(4,1)S(1)}, s32[]{:S(2)}) async-start(s8[7077888]{0:T(1024)(128)(4,1)} %bitcast.68), calls=%async_computation.1 | async-start | bytes 5767168
  30.0 18.7 %copy-start.10 = (f32[128,64]{0,1:T(8,128)}, f32[128,64]{0,1:T(8,128)S(1)}, u32[]{:S(2)}) copy-start(f32[128,64]{0,1:T(8,128)S(1)} %slice.41) | copy-start | bytes 98308
  30.1 11.8 %collective-permute-start.6 = (f32[128,576]{0,1:T(8,128)S(1)}, f32[128,576]{0,1:T(8,128)S(1)}, u32[]{:S(2)}, u32[]{:S(2)}) collective-permute-start(f32[128,576]{0,1:T(8,128)S(1)} %pad_maximum_fusion.3), channel_id=1, source_target_pairs={{0,24},{1,25},{2,26},{3,27},{4,28},{5,29},{6,30},{7,31}} | collective-permute-start | bytes 884744 | tf_op jit(solution)/shard_map/ppermute | solution.py:78
  34.5 14.2 %collective-permute-start.5 = (f32[128,576]{0,1:T(8,128)S(1)}, f32[128,576]{0,1:T(8,128)S(1)}, u32[]{:S(2)}, u32[]{:S(2)}) collective-permute-start(f32[128,576]{0,1:T(8,128)S(1)} %pad_maximum_fusion.3), channel_id=1, source_target_pairs={{0,16},{8,24},{1,17},{9,25},{2,18},{10,26},{3,19},{11,27},{4,20},{... | collective-permute-start | bytes 884744 | tf_op jit(solution)/shard_map/ppermute | solution.py:78
  35.8 12.9 %collective-permute-start.4 = (f32[128,576]{0,1:T(8,128)S(1)}, f32[128,576]{0,1:T(8,128)S(1)}, u32[]{:S(2)}, u32[]{:S(2)}) collective-permute-start(f32[128,576]{0,1:T(8,128)S(1)} %pad_maximum_fusion.3), channel_id=1, source_target_pairs={{0,8},{8,16},{16,24},{1,9},{9,17},{17,25},{2,10},{10,18},{18,26},{... | collective-permute-start | bytes 884744 | tf_op jit(solution)/shard_map/ppermute | solution.py:78
  41.9 6.9 %copy-start.2 = (f32[128,576]{0,1:T(8,128)}, f32[128,576]{0,1:T(8,128)S(1)}, u32[]{:S(2)}) copy-start(f32[128,576]{0,1:T(8,128)S(1)} %collective-permute-done.6) | copy-start | bytes 884740
  48.7 0.8 copy-start.6
  57.6 1.0 %copy-start.3 = (f32[128,576]{0,1:T(8,128)S(1)}, f32[128,576]{0,1:T(8,128)}, u32[]{:S(2)}) copy-start(f32[128,576]{0,1:T(8,128)} %copy-done.2) | copy-start | bytes 884740
  57.6 1.0 %copy-start.5 = (f32[128,576]{0,1:T(8,128)S(1)}, f32[128,576]{0,1:T(8,128)}, u32[]{:S(2)}) copy-start(f32[128,576]{0,1:T(8,128)} %copy-done.4) | copy-start | bytes 884740
  57.6 1.1 %copy-start.7 = (f32[128,576]{0,1:T(8,128)S(1)}, f32[128,576]{0,1:T(8,128)}, u32[]{:S(2)}) copy-start(f32[128,576]{0,1:T(8,128)} %copy-done.6) | copy-start | bytes 884740
  57.6 1.1 %copy-start.9 = (pred[128,512]{1,0:T(8,128)(4,1)S(1)}, pred[128,512]{1,0:T(8,128)(4,1)}, u32[]{:S(2)}) copy-start(pred[128,512]{1,0:T(8,128)(4,1)} %and_and_fusion) | copy-start | bytes 196612
  57.6 1.1 %copy-start.11 = (f32[128,64]{0,1:T(8,128)S(1)}, f32[128,64]{0,1:T(8,128)}, u32[]{:S(2)}) copy-start(f32[128,64]{0,1:T(8,128)} %copy-done.10) | copy-start | bytes 98308
  66.1 2.3 %collective-permute-start.7 = (f32[4,16,2304]{2,1,0:T(8,128)}, f32[4,16,2304]{2,1,0:T(8,128)}, u32[]{:S(2)}, u32[]{:S(2)}) collective-permute-start(f32[4,16,2304]{2,1,0:T(8,128)} %dynamic-slice_bitcast_fusion), channel_id=1, source_target_pairs={{0,1},{1,0},{2,3},{3,2},{4,5},{5,4},{6,7},{7,6},{8,9},{9,8},{10,11... | collective-permute-start | bytes 1769480 | tf_op jit(solution)/shard_map/ppermute | solution.py:24
  69.6 7.2 %collective-permute-start.10 = (f32[16,2304]{1,0:T(8,128)S(1)}, f32[16,2304]{1,0:T(8,128)S(1)}, u32[]{:S(2)}, u32[]{:S(2)}) collective-permute-start(f32[16,2304]{1,0:T(8,128)S(1)} %get-tuple-element.9), channel_id=1, source_target_pairs={{0,6},{1,7},{2,0},{3,1},{4,2},{5,3},{6,4},{7,5},{8,14},{9,15},{10,... | collective-permute-start | bytes 442376 | tf_op jit(solution)/shard_map/ppermute | solution.py:29
  72.5 14.5 %collective-permute-start.9 = (f32[16,2304]{1,0:T(8,128)S(1)}, f32[16,2304]{1,0:T(8,128)S(1)}, u32[]{:S(2)}, u32[]{:S(2)}) collective-permute-start(f32[16,2304]{1,0:T(8,128)S(1)} %get-tuple-element.10), channel_id=1, source_target_pairs={{0,4},{1,5},{2,6},{3,7},{4,0},{5,1},{6,2},{7,3},{8,12},{9,13},{10,... | collective-permute-start | bytes 442376 | tf_op jit(solution)/shard_map/ppermute | solution.py:29
  73.6 13.3 %collective-permute-start.8 = (f32[16,2304]{1,0:T(8,128)S(1)}, f32[16,2304]{1,0:T(8,128)S(1)}, u32[]{:S(2)}, u32[]{:S(2)}) collective-permute-start(f32[16,2304]{1,0:T(8,128)S(1)} %get-tuple-element.8), channel_id=1, source_target_pairs={{0,2},{1,3},{2,4},{3,5},{4,6},{5,7},{6,0},{7,1},{8,10},{9,11},{10,... | collective-permute-start | bytes 442376 | tf_op jit(solution)/shard_map/ppermute | solution.py:29
  (1 other events, 0.7 us)

commit v2 on v1

v2 whole, which is shorter than its diff:
```python
import functools
import math

import jax
import jax.numpy as jnp
from jax import lax
from jax.experimental import pallas as pl
from jax.experimental.pallas import tpu as pltpu
from jax.sharding import PartitionSpec as P

KV_RANK = 512
NOPE = 128
ROPE = 64
VDIM = 128
QK = NOPE + ROPE

eps_norm = 1e-06
neg_fill = -1e30
F32 = jnp.float32
BF16 = jnp.bfloat16
VM = pl.BlockSpec(memory_space=pltpu.VMEM)
SM = pl.BlockSpec(memory_space=pltpu.SMEM)
NT = (((1,), (1,)), ((), ()))
NN = (((1,), (0,)), ((), ()))


def split(value):
    high = value.astype(BF16)
    return high, (value - high.astype(F32)).astype(BF16)


def dot3(left, right, dims=NN):
    rows = left[0].shape[0]
    stacked = lax.dot_general(
        jnp.concatenate(left, axis=0), right[0], dims, preferred_element_type=F32
    )
    rest = lax.dot_general(left[0], right[1], dims, preferred_element_type=F32)
    return stacked[:rows] + (stacked[rows:] + rest)


def latent_kernel(x_ref, w_ref, o_ref, acc):
    at = pl.program_id(0)

    @pl.when(at == 0)
    def _():
        acc[...] = jnp.zeros_like(acc)

    acc[...] += dot3(split(x_ref[...]), split(w_ref[...]), NT)

    @pl.when(at == pl.num_programs(0) - 1)
    def _():
        raw = acc[...]
        part = raw[:, :KV_RANK]
        mean_square = jnp.mean(part * part, axis=1, keepdims=True)
        o_ref[:, :KV_RANK] = part * lax.rsqrt(mean_square + eps_norm)
        o_ref[:, KV_RANK:] = raw[:, KV_RANK:]


def own_latent(x, w_down):
    rows, depth = x.shape
    wide = w_down.shape[1]
    step = depth // 3
    return pl.pallas_call(
        latent_kernel,
        grid=(3,),
        in_specs=[
            pl.BlockSpec((rows, step), lambda i: (0, i)),
            pl.BlockSpec((wide, step), lambda i: (0, i)),
        ],
        out_specs=pl.BlockSpec((rows, wide), lambda i: (0, 0)),
        out_shape=jax.ShapeDtypeStruct((rows, wide), F32),
        scratch_shapes=[pltpu.VMEM((rows, wide), F32)],
        compiler_params=pltpu.CompilerParams(vmem_limit_bytes=12 << 20),
        cost_estimate=pl.CostEstimate(
            flops=6 * rows * depth * wide, bytes_accessed=4 * depth * wide, transcendentals=0
        ),
        name="own_latent",
    )(x, w_down.T)


def keys_kernel(count, hc, *refs):
    lat = refs[:count]
    w_ref, kh_ref, kl_ref, vh_ref, vl_ref, wh, wl = refs[count:]
    wh[...], wl[...] = split(w_ref[...])
    weight = (wh[...], wl[...])
    at = 0
    for ref in lat:
        rows = ref.shape[0]
        up = dot3(split(ref[:, :KV_RANK]), weight)
        sh, sl = split(ref[:, KV_RANK:])
        for h in range(hc):
            base = h * (NOPE + VDIM)
            high, low = split(up[:, base : base + NOPE])
            kh_ref[h, at : at + rows, :NOPE] = high
            kl_ref[h, at : at + rows, :NOPE] = low
            kh_ref[h, at : at + rows, NOPE:] = sh
            kl_ref[h, at : at + rows, NOPE:] = sl
            high, low = split(up[:, base + NOPE : base + NOPE + VDIM])
            vh_ref[h, at : at + rows, :] = high
            vl_ref[h, at : at + rows, :] = low
        at += rows


def keys_values(latents, w_up):
    hc = w_up.shape[1] // (NOPE + VDIM)
    total = sum(a.shape[0] for a in latents)
    key = jax.ShapeDtypeStruct((hc, total, QK), BF16)
    val = jax.ShapeDtypeStruct((hc, total, VDIM), BF16)
    return pl.pallas_call(
        functools.partial(keys_kernel, len(latents), hc),
        in_specs=[VM] * (len(latents) + 1),
        out_specs=[VM] * 4,
        out_shape=[key, key, val, val],
        scratch_shapes=[pltpu.VMEM(w_up.shape, BF16)] * 2,
        compiler_params=pltpu.CompilerParams(vmem_limit_bytes=24 << 20),
        cost_estimate=pl.CostEstimate(
            flops=6 * total * KV_RANK * w_up.shape[1], bytes_accessed=4 << 20, transcendentals=0
        ),
        name="keys_values",
    )(*latents, w_up)


def attend_kernel(chips, ctx_count, hc, rows, *refs):
    blocks = refs[: 2 * chips]
    (w_ref, at_ref, kh_ref, kl_ref, vh_ref, vl_ref, o_ref, n_ref, xs, acc) = refs[2 * chips :]
    step = pl.program_id(0)
    chip, core, ctx, cut = at_ref[0], at_ref[1], at_ref[2], at_ref[3]
    size = rows * 2 * chips

    for n, ref in enumerate(blocks):
        other, s = n // chips, n % chips
        src = 2 * lax.rem(chip - s + chips, chips) + (core if other == 0 else 1 - core)
        high, low = split(ref[...])
        place = pl.multiple_of(src * rows, rows)
        xs[pl.ds(place, rows), :] = high
        xs[pl.ds(size + place, rows), :] = low
    wh, wl = split(w_ref[...])
    stacked = jnp.dot(xs[...], wh, preferred_element_type=F32)
    part = stacked[:size] + (stacked[size:] + jnp.dot(xs[:size], wl, preferred_element_type=F32))

    @pl.when(step == 0)
    def _():
        acc[...] = part

    @pl.when(step > 0)
    def _():
        acc[...] += part

    @pl.when(step == pl.num_programs(0) - 1)
    def _():
        total_keys = kh_ref.shape[1]
        half = rows * chips
        idx = lax.broadcasted_iota(jnp.int32, (1, total_keys), 1)
        which = idx // half
        shard_slot = lax.rem(which, ctx_count)
        flip = which // ctx_count
        inside = lax.rem(idx, half)
        src = lax.rem(chip - inside // rows + chips, chips)
        src = 2 * src + (core ^ flip)
        key_pos = (ctx ^ shard_slot) * size + src * rows + lax.rem(inside, rows)
        query_pos = ctx * size + lax.broadcasted_iota(jnp.int32, (size, 1), 0)
        allowed = (key_pos <= query_pos) & ((key_pos >= cut) | (query_pos < cut))
        factor = 1.0 / math.sqrt(QK)
        for h in range(hc):
            q = split(acc[:, h * QK : (h + 1) * QK])
            scores = dot3(q, (kh_ref[h], kl_ref[h]), NT) * factor
            scores = jnp.where(allowed, scores, neg_fill)
            peak = jnp.max(scores, axis=1, keepdims=True)
            weights = jnp.where(allowed, jnp.exp(scores - peak), 0.0)
            total = jnp.sum(weights, axis=1, keepdims=True)
            out = dot3(split(weights), (vh_ref[h], vl_ref[h]))
            o_ref[:, h * VDIM : (h + 1) * VDIM] = out / total
            n_ref[:, h : h + 1] = peak + jnp.log(total)


def attend(blocks, place, w_query, keys):
    hc = keys[0].shape[0]
    rows, depth = blocks[0].shape
    chips = len(blocks) // 2
    size = rows * len(blocks)
    total_keys = keys[0].shape[1]
    wide = w_query.shape[1]
    steps = 3
    part = depth // steps
    return pl.pallas_call(
        functools.partial(attend_kernel, chips, total_keys // size, hc, rows),
        grid=(steps,),
        in_specs=[pl.BlockSpec((rows, part), lambda i: (0, i))] * len(blocks)
        + [pl.BlockSpec((part, wide), lambda i: (i, 0)), SM]
        + [VM] * 4,
        out_specs=[
            pl.BlockSpec((size, hc * VDIM), lambda i: (0, 0)),
            pl.BlockSpec((size, hc), lambda i: (0, 0)),
        ],
        out_shape=[
            jax.ShapeDtypeStruct((size, hc * VDIM), F32),
            jax.ShapeDtypeStruct((size, hc), F32),
        ],
        scratch_shapes=[pltpu.VMEM((2 * size, part), BF16), pltpu.VMEM((size, wide), F32)],
        compiler_params=pltpu.CompilerParams(vmem_limit_bytes=40 << 20),
        cost_estimate=pl.CostEstimate(
            flops=6 * size * depth * wide, bytes_accessed=12 << 20, transcendentals=0
        ),
        name="attend",
    )(*blocks, w_query, place, *keys)


def project_kernel(chips, rows, x_ref, w_ref, at_ref, give_ref, keep_ref, acc):
    chip, core = at_ref[0], at_ref[1]
    acc[...] = dot3(split(x_ref[...]), split(w_ref[...]))
    for s in range(chips):
        dst = 2 * lax.rem(chip + s, chips)
        mine = pl.multiple_of((dst + core) * rows, rows)
        theirs = pl.multiple_of((dst + 1 - core) * rows, rows)
        keep_ref[s * rows : (s + 1) * rows, :] = acc[pl.ds(mine, rows), :]
        give_ref[s * rows : (s + 1) * rows, :] = acc[pl.ds(theirs, rows), :]


def project(x, place, w_out, chips):
    size, depth = x.shape
    wide = w_out.shape[1]
    rows = size // (2 * chips)
    steps = 3
    part = wide // steps
    half = jax.ShapeDtypeStruct((size // 2, wide), F32)
    return pl.pallas_call(
        functools.partial(project_kernel, chips, rows),
        grid=(steps,),
        in_specs=[
            pl.BlockSpec((size, depth), lambda i: (0, 0)),
            pl.BlockSpec((depth, part), lambda i: (0, i)),
            SM,
        ],
        out_specs=[pl.BlockSpec((size // 2, part), lambda i: (0, i))] * 2,
        out_shape=[half, half],
        scratch_shapes=[pltpu.VMEM((size, part), F32)],
        compiler_params=pltpu.CompilerParams(vmem_limit_bytes=24 << 20),
        cost_estimate=pl.CostEstimate(
            flops=6 * size * depth * wide, bytes_accessed=8 << 20, transcendentals=0
        ),
        name="project",
    )(x, w_out, place)


def partner_swap(value):
    count = lax.axis_size("head")
    return lax.ppermute(value, "head", [(i, i ^ 1) for i in range(count)])


def chip_shift(value, step):
    count = lax.axis_size("head")
    return lax.ppermute(value, "head", [(i, (i + 2 * step) % count) for i in range(count)])


def shard_send(value, flip):
    count = lax.axis_size("ctx")
    pairs = [(i, i ^ flip) for i in range(count) if i < i ^ flip < count]
    return lax.ppermute(value, "ctx", pairs)


def body(hidden_rows, segment_ids, w_query, w_down, w_up, w_out):
    ctx_count = lax.axis_size("ctx")
    chips = lax.axis_size("head") // 2
    ctx_at = lax.axis_index("ctx")
    me = lax.axis_index("head")
    cut = jnp.sum((segment_ids == 0).astype(jnp.int32))
    place = jnp.stack([me // 2, me % 2, ctx_at, cut]).astype(jnp.int32)
    rows = hidden_rows.shape[0]

    mine = [hidden_rows] + [chip_shift(hidden_rows, s) for s in range(1, chips)]
    latent = own_latent(hidden_rows, w_down)
    column = jnp.concatenate([latent] + [chip_shift(latent, s) for s in range(1, chips)])
    lat = [column] + [shard_send(column, f) for f in range(1, ctx_count)]
    keys = keys_values(lat + [partner_swap(a) for a in lat], w_up)
    blocks = mine + [partner_swap(a) for a in mine]
    out, norm = attend(blocks, place, w_query, keys)
    give, keep = project(out, place, w_out, chips)
    pair = keep + partner_swap(give)
    total = pair[:rows]
    for s in range(1, chips):
        total = total + chip_shift(pair[s * rows : (s + 1) * rows], s)
    return (total, norm.T)


def solution(mesh):
    in_specs = (
        P(("ctx", "head"), None),
        P(),
        P(None, "head"),
        P(),
        P(None, "head"),
        P("head", None),
    )
    out_specs = (P(("ctx", "head"), None), P("head", "ctx"))
    return jax.shard_map(body, mesh=mesh, in_specs=in_specs, out_specs=out_specs, check_vma=False)
```

time: 88.1 us -> 66.4 us (0.75)
  matrix products: 17.5 us -> 0 us
  Pallas kernels: 0 us -> 15.1 us
  local copies, waits for them, and re-layouts: 20.8 us -> 6.22 us
  waiting for transfers between devices: 22.9 us -> 13.5 us
  starting transfers between devices: 19.2 us -> 27.6 us
  other arithmetic: 6.22 us -> 2.12 us
    dot_general x7 -> x0, matrix products: 17.5 us -> none  [the longest x4 14.9 us: product(): jnp.dot(left, right, precision=precise, preferred_element_type=jnp.float32)]
    pallas_call x0 -> x4, Pallas kernels: none -> 15.1 us  [the longest x1 5.31 us: attend(): pl.pallas_call(functools.partial(attend_kernel, chips, total_keys // size...]
    ppermute x3, waiting for transfers between devices: 7.1 us -> 0.01 us  [shard_send(): return lax.ppermute(value, 'ctx', pairs)]
    ppermute x6 -> x9, starting transfers between devices: 10.8 us -> 16.4 us  [chip_shift(): lax.ppermute(value, 'head', [(i, (i + 2 * step) % count) for i in range(c...]
    gather x2 -> x0, local copies, waits for them, and re-layouts: 5.37 us -> none  [the longest x1 3.48 us: body(): key_seg = jnp.take(segment_ids, jnp.maximum(key_pos, 0))]
    reshape x1 -> x0, local copies, waits for them, and re-layouts: 3.14 us -> none  [body(): product(keys_all[:, :KV_RANK], w_up).reshape(-1, head_count, NOPE + VDIM)]
    unnamed x29 -> x13, local copies, waits for them, and re-layouts: 9.22 us -> 6.19 us
    ppermute x2 -> x9, starting transfers between devices: 0.01 us -> 2.18 us  [partner_swap(): return lax.ppermute(value, 'head', [(i, i ^ 1) for i in range(count)])]
  transfers between devices with their start and end apart: 11 -> 21, of which waited for: 6 -> 6; matrix products, arithmetic and copies ran while one was open for 18% -> 3% of each run, Pallas kernels for 0% -> 6%
where the time goes in v2:
time: 66.4 us; the launch traced here: 65.3 us
  starting transfers between devices  27.6 us (42%)
  Pallas kernels  15.1 us (23%)
  waiting for transfers between devices  13.5 us (20%)
  local copies, waits for them, and re-layouts  6.22 us (9%)
  other arithmetic  2.12 us (3%)
  between operations  0.78 us (1%)
    ppermute x9, starting transfers between devices, chip_shift(): lax.ppermute(value, 'head', [(i, (i + 2 * step) % count) for i in range(c...  16.4 us
    ppermute x9, waiting for transfers between devices, chip_shift(): lax.ppermute(value, 'head', [(i, (i + 2 * step) % count) for i in range(c...  11.6 us
    ppermute x3, starting transfers between devices, shard_send(): return lax.ppermute(value, 'ctx', pairs)  8.94 us
    unnamed x13, local copies, waits for them, and re-layouts  6.19 us
    pallas_call x1, Pallas kernels, attend(): pl.pallas_call(functools.partial(attend_kernel, chips, total_keys // size...  5.31 us
    pallas_call x1, Pallas kernels, keys_values(): pl.pallas_call(functools.partial(keys_kernel, len(latents), hc), in_specs...  4.2 us
    pallas_call x1, Pallas kernels, own_latent(): pl.pallas_call(latent_kernel, grid=(3,), in_specs=[pl.BlockSpec((rows, st...  3.09 us
    pallas_call x1, Pallas kernels, project(): pl.pallas_call(functools.partial(project_kernel, chips, rows), grid=(step...  2.46 us
  transfers between devices with their start and end apart: 21, of which 6 were waited for; matrix products, arithmetic and copies ran while one was open for 3% of the time, Pallas kernels for 6%

profile of v2, /device:TPU:0, one launch (start us, length us, event | category | flops | bytes accessed | tf_op | source)
XLA Modules:
  0.0 65.3 jit_solution(10679776823778043377)
XLA Ops:
  0.6 2.5 %copy-done.1 = f32[2304,576]{0,1:T(8,128)S(1)} copy-done((f32[2304,576]{0,1:T(8,128)S(1)}, f32[2304,576]{0,1:T(8,128)}, u32[]{:S(2)}) %copy-start.1) | copy-done | bytes 5308440
  3.1 3.1 %own_latent.1 = f32[16,576]{1,0:T(8,128)S(1)} custom-call(f32[16,2304]{1,0:T(8,128)} %refs_0_.1, f32[576,2304]{1,0:T(8,128)S(1)} %bitcast.6), custom_call_target="tpu_custom_call" | custom-call | flops 127401984 | bytes 5308416 | tf_op jit(solution)/shard_map/own_latent/pallas_call | solution.py:63
  6.2 3.1 %collective-permute-start.7 = (f32[16,576]{1,0:T(8,128)S(1)}, f32[16,576]{1,0:T(8,128)S(1)}, u32[]{:S(2)}, u32[]{:S(2)}) collective-permute-start(f32[16,576]{1,0:T(8,128)S(1)} %own_latent.1), channel_id=1, source_target_pairs={{0,2},{1,3},{2,4},{3,5},{4,6},{5,7},{6,0},{7,1},{8,10},{9,11},{10,... | collective-permute-start | bytes 110600 | tf_op jit(solution)/shard_map/ppermute | solution.py:252
  9.3 2.6 %collective-permute-start.8 = (f32[16,576]{1,0:T(8,128)S(1)}, f32[16,576]{1,0:T(8,128)S(1)}, u32[]{:S(2)}, u32[]{:S(2)}) collective-permute-start(f32[16,576]{1,0:T(8,128)S(1)} %own_latent.1), channel_id=1, source_target_pairs={{0,4},{1,5},{2,6},{3,7},{4,0},{5,1},{6,2},{7,3},{8,12},{9,13},{10,... | collective-permute-start | bytes 110600 | tf_op jit(solution)/shard_map/ppermute | solution.py:252
  11.9 1.4 %collective-permute-start.9 = (f32[16,576]{1,0:T(8,128)S(1)}, f32[16,576]{1,0:T(8,128)S(1)}, u32[]{:S(2)}, u32[]{:S(2)}) collective-permute-start(f32[16,576]{1,0:T(8,128)S(1)} %own_latent.1), channel_id=1, source_target_pairs={{0,6},{1,7},{2,0},{3,1},{4,2},{5,3},{6,4},{7,5},{8,14},{9,15},{10,... | collective-permute-start | bytes 110600 | tf_op jit(solution)/shard_map/ppermute | solution.py:252
  13.3 0.7 %collective-permute-start = (f32[16,2304]{1,0:T(8,128)}, f32[16,2304]{1,0:T(8,128)S(1)}, u32[]{:S(2)}, u32[]{:S(2)}) collective-permute-start(f32[16,2304]{1,0:T(8,128)} %refs_0_.1), channel_id=1, source_target_pairs={{0,2},{1,3},{2,4},{3,5},{4,6},{5,7},{6,0},{7,1},{8,10},{9,11},{10,... | collective-permute-start | bytes 442376 | tf_op jit(solution)/shard_map/ppermute | solution.py:252
  14.7 1.2 %collective-permute-done.9 = f32[16,576]{1,0:T(8,128)S(1)} collective-permute-done((f32[16,576]{1,0:T(8,128)S(1)}, f32[16,576]{1,0:T(8,128)S(1)}, u32[]{:S(2)}, u32[]{:S(2)}) %collective-permute-start.9) | collective-permute-done | bytes 36896 | tf_op jit(solution)/shard_map/ppermute | solution.py:252
  15.9 3.5 %collective-permute-start.10 = (f32[64,576]{1,0:T(8,128)S(1)}, f32[64,576]{1,0:T(8,128)S(1)}, u32[]{:S(2)}, u32[]{:S(2)}) collective-permute-start(f32[64,576]{1,0:T(8,128)S(1)} %pad_maximum_fusion.refs_0_), channel_id=1, source_target_pairs={{0,8},{16,24},{1,9},{17,25},{2,10},{18,26},{3,11},{19,27},{4,12},{... | collective-permute-start | bytes 442376 | tf_op jit(solution)/shard_map/ppermute | solution.py:258
  19.5 3.4 %collective-permute-start.11 = (f32[64,576]{1,0:T(8,128)S(1)}, f32[64,576]{1,0:T(8,128)S(1)}, u32[]{:S(2)}, u32[]{:S(2)}) collective-permute-start(f32[64,576]{1,0:T(8,128)S(1)} %pad_maximum_fusion.refs_0_), channel_id=1, source_target_pairs={{0,16},{8,24},{1,17},{9,25},{2,18},{10,26},{3,19},{11,27},{4,20},{... | collective-permute-start | bytes 442376 | tf_op jit(solution)/shard_map/ppermute | solution.py:258
  22.9 2.0 %collective-permute-start.12 = (f32[64,576]{1,0:T(8,128)S(1)}, f32[64,576]{1,0:T(8,128)}, u32[]{:S(2)}, u32[]{:S(2)}) collective-permute-start(f32[64,576]{1,0:T(8,128)S(1)} %pad_maximum_fusion.refs_0_), channel_id=1, source_target_pairs={{0,24},{8,16},{1,25},{9,17},{2,26},{10,18},{3,27},{11,19},{4,28},{... | collective-permute-start | bytes 442376 | tf_op jit(solution)/shard_map/ppermute | solution.py:258
  24.9 3.6 %collective-permute-start.2 = (f32[16,2304]{1,0:T(8,128)}, f32[16,2304]{1,0:T(8,128)S(1)}, u32[]{:S(2)}, u32[]{:S(2)}) collective-permute-start(f32[16,2304]{1,0:T(8,128)} %refs_0_.1), channel_id=1, source_target_pairs={{0,6},{1,7},{2,0},{3,1},{4,2},{5,3},{6,4},{7,5},{8,14},{9,15},{10,... | collective-permute-start | bytes 442376 | tf_op jit(solution)/shard_map/ppermute | solution.py:252
  29.5 0.6 convert_reduce_fusion
  30.1 0.7 %pad_add_fusion.refs_9_.at_ref = s32[4]{0:T(128)S(1)} fusion(s32[1]{0:T(128)} %bitcast.3, s32[1]{0:T(128)} %bitcast.2, s32[1]{0:T(128)} %bitcast.1, s32[1]{0:T(128)} %bitcast), kind=kLoop, calls=%fused_computation.5 | loop fusion | flops 12 | bytes 32 | tf_op jit(solution)/shard_map/stack | solution.py:267
  32.5 4.2 %keys_values.1 = (bf16[4,512,192]{2,1,0:T(8,128)(2,1)S(1)}, bf16[4,512,192]{2,1,0:T(8,128)(2,1)S(1)}, bf16[4,512,128]{2,1,0:T(8,128)(2,1)S(1)}, bf16[4,512,128]{2,1,0:T(8,128)(2,1)S(1)}) custom-call(f32[64,576]{1,0:T(8,128)S(1)} %pad_maximum_fusion.refs_0_, f32[64,576]{1,0:T(8,128)S(1)} %collective-permute-done.10.refs_1_, ...), custom_call_target="tpu_custom_call" | custom-call | flops 1610612736 | bytes 4194304 | tf_op jit(solution)/shard_map/keys_values/pallas_call | solution.py:109
  36.8 3.0 %copy-done = f32[2304,768]{1,0:T(8,128)S(1)} copy-done((f32[2304,768]{1,0:T(8,128)S(1)}, f32[2304,768]{1,0:T(8,128)}, u32[]{:S(2)}) %copy-start) | copy-done | bytes 7077912
  39.8 5.3 %attend.1 = (f32[128,512]{1,0:T(8,128)S(1)}, f32[128,4]{1,0:T(8,128)S(1)}) custom-call(f32[16,2304]{1,0:T(8,128)} %refs_0_.1, f32[16,2304]{1,0:T(8,128)S(1)} %collective-permute-done.refs_1_, f32[16,2304]{1,0:T(8,128)S(1)} %collective-permute-done.1.refs_2_, f32[16,2304]{1,0:T(8,128)S(1)} %collective-permute-done.2.refs_3_, ...), custom_call_target="tpu_custom_call" | custom-call | flops 1358954496 | bytes 12582912 | tf_op jit(solution)/shard_map/attend/pallas_call | solution.py:185
  45.1 2.5 %project.1 = (f32[64,2304]{1,0:T(8,128)S(1)}, f32[64,2304]{1,0:T(8,128)S(1)}) custom-call(f32[128,512]{1,0:T(8,128)S(1)} %get-tuple-element.14.x_ref, f32[512,2304]{1,0:T(8,128)S(1)} %bitcast.8, s32[4]{0:T(128)S(1)} %pad_add_fusion.refs_9_.at_ref), custom_call_target="tpu_custom_call" | custom-call | flops 905969664 | bytes 8388608 | tf_op jit(solution)/shard_map/project/pallas_call | solution.py:226
  47.7 1.9 %collective-permute-done.17 = f32[64,2304]{1,0:T(8,128)S(1)} collective-permute-done((f32[64,2304]{1,0:T(8,128)S(1)}, f32[64,2304]{1,0:T(8,128)S(1)}, u32[]{:S(2)}, u32[]{:S(2)}) %collective-permute-start.17) | collective-permute-done | bytes 589856 | tf_op jit(solution)/shard_map/ppermute | solution.py:247
  49.8 0.9 %collective-permute-start.18 = (f32[16,2304]{1,0:T(8,128)S(1)}, f32[16,2304]{1,0:T(8,128)S(1)}, u32[]{:S(2)}, u32[]{:S(2)}) collective-permute-start(f32[16,2304]{1,0:T(8,128)S(1)} %get-tuple-element.20), channel_id=1, source_target_pairs={{0,2},{1,3},{2,4},{3,5},{4,6},{5,7},{6,0},{7,1},{8,10},{9,11},{10,... | collective-permute-start | bytes 442376 | tf_op jit(solution)/shard_map/ppermute | solution.py:252
  50.7 3.9 %collective-permute-start.19 = (f32[16,2304]{1,0:T(8,128)S(1)}, f32[16,2304]{1,0:T(8,128)S(1)}, u32[]{:S(2)}, u32[]{:S(2)}) collective-permute-start(f32[16,2304]{1,0:T(8,128)S(1)} %get-tuple-element.22), channel_id=1, source_target_pairs={{0,4},{1,5},{2,6},{3,7},{4,0},{5,1},{6,2},{7,3},{8,12},{9,13},{10,... | collective-permute-start | bytes 442376 | tf_op jit(solution)/shard_map/ppermute | solution.py:252
  54.6 0.7 copy.8
  55.2 3.6 %collective-permute-done.18 = f32[16,2304]{1,0:T(8,128)S(1)} collective-permute-done((f32[16,2304]{1,0:T(8,128)S(1)}, f32[16,2304]{1,0:T(8,128)S(1)}, u32[]{:S(2)}, u32[]{:S(2)}) %collective-permute-start.18) | collective-permute-done | bytes 147488 | tf_op jit(solution)/shard_map/ppermute | solution.py:252
  58.8 5.7 %collective-permute-done.19 = f32[16,2304]{1,0:T(8,128)S(1)} collective-permute-done((f32[16,2304]{1,0:T(8,128)S(1)}, f32[16,2304]{1,0:T(8,128)S(1)}, u32[]{:S(2)}, u32[]{:S(2)}) %collective-permute-start.19) | collective-permute-done | bytes 147488 | tf_op jit(solution)/shard_map/ppermute | solution.py:252
  64.6 0.7 %fusion.1 = f32[16,2304]{1,0:T(8,128)} fusion(f32[16,2304]{1,0:T(8,128)S(1)} %collective-permute-done.20, f32[16,2304]{1,0:T(8,128)S(1)} %collective-permute-done.19, f32[16,2304]{1,0:T(8,128)S(1)} %collective-permute-done.18, f32[64,2304]{1,0:T(8,128)S(1)} %add.18), kind=kLoop, calls=%fused_computation.3 | loop fusion | flops 110592 | bytes 737280 | tf_op jit(solution)/shard_map/add | solution.py:281
  (42 shorter events, 3.7 us)
Async XLA Ops:
  3.1 26.4 %copy-start.3 = (s32[512]{0:T(512)S(1)}, s32[512]{0:T(512)}, u32[]{:S(2)}) copy-start(s32[512]{0:T(512)} %param.7) | copy-start | bytes 6148
  3.1 29.4 %copy-start.2 = (f32[512,1024]{1,0:T(8,128)S(1)}, f32[512,1024]{1,0:T(8,128)}, u32[]{:S(2)}) copy-start(f32[512,1024]{1,0:T(8,128)} %refs_8_.2) | copy-start | bytes 6291460
  6.2 8.0 %collective-permute-start.7 = (f32[16,576]{1,0:T(8,128)S(1)}, f32[16,576]{1,0:T(8,128)S(1)}, u32[]{:S(2)}, u32[]{:S(2)}) collective-permute-start(f32[16,576]{1,0:T(8,128)S(1)} %own_latent.1), channel_id=1, source_target_pairs={{0,2},{1,3},{2,4},{3,5},{4,6},{5,7},{6,0},{7,1},{8,10},{9,11},{10,... | collective-permute-start | bytes 110600 | tf_op jit(solution)/shard_map/ppermute | solution.py:252
  9.3 5.4 %collective-permute-start.8 = (f32[16,576]{1,0:T(8,128)S(1)}, f32[16,576]{1,0:T(8,128)S(1)}, u32[]{:S(2)}, u32[]{:S(2)}) collective-permute-start(f32[16,576]{1,0:T(8,128)S(1)} %own_latent.1), channel_id=1, source_target_pairs={{0,4},{1,5},{2,6},{3,7},{4,0},{5,1},{6,2},{7,3},{8,12},{9,13},{10,... | collective-permute-start | bytes 110600 | tf_op jit(solution)/shard_map/ppermute | solution.py:252
  11.9 4.0 %collective-permute-start.9 = (f32[16,576]{1,0:T(8,128)S(1)}, f32[16,576]{1,0:T(8,128)S(1)}, u32[]{:S(2)}, u32[]{:S(2)}) collective-permute-start(f32[16,576]{1,0:T(8,128)S(1)} %own_latent.1), channel_id=1, source_target_pairs={{0,6},{1,7},{2,0},{3,1},{4,2},{5,3},{6,4},{7,5},{8,14},{9,15},{10,... | collective-permute-start | bytes 110600 | tf_op jit(solution)/shard_map/ppermute | solution.py:252
  13.3 11.6 %collective-permute-start = (f32[16,2304]{1,0:T(8,128)}, f32[16,2304]{1,0:T(8,128)S(1)}, u32[]{:S(2)}, u32[]{:S(2)}) collective-permute-start(f32[16,2304]{1,0:T(8,128)} %refs_0_.1), channel_id=1, source_target_pairs={{0,2},{1,3},{2,4},{3,5},{4,6},{5,7},{6,0},{7,1},{8,10},{9,11},{10,... | collective-permute-start | bytes 442376 | tf_op jit(solution)/shard_map/ppermute | solution.py:252
  13.9 14.5 %collective-permute-start.1 = (f32[16,2304]{1,0:T(8,128)}, f32[16,2304]{1,0:T(8,128)S(1)}, u32[]{:S(2)}, u32[]{:S(2)}) collective-permute-start(f32[16,2304]{1,0:T(8,128)} %refs_0_.1), channel_id=1, source_target_pairs={{0,4},{1,5},{2,6},{3,7},{4,0},{5,1},{6,2},{7,3},{8,12},{9,13},{10,... | collective-permute-start | bytes 442376 | tf_op jit(solution)/shard_map/ppermute | solution.py:252
  15.9 29.2 %slice-start = ((s8[4718592]{0:T(1024)(128)(4,1)}), s8[524288]{0:T(1024)(128)(4,1)S(1)}, s32[]{:S(2)}) async-start(s8[4718592]{0:T(1024)(128)(4,1)} %bitcast.7), calls=%async_computation | async-start | bytes 1048576
  15.9 12.6 %collective-permute-start.10 = (f32[64,576]{1,0:T(8,128)S(1)}, f32[64,576]{1,0:T(8,128)S(1)}, u32[]{:S(2)}, u32[]{:S(2)}) collective-permute-start(f32[64,576]{1,0:T(8,128)S(1)} %pad_maximum_fusion.refs_0_), channel_id=1, source_target_pairs={{0,8},{16,24},{1,9},{17,25},{2,10},{18,26},{3,11},{19,27},{4,12},{... | collective-permute-start | bytes 442376 | tf_op jit(solution)/shard_map/ppermute | solution.py:258
  19.5 9.5 %collective-permute-start.11 = (f32[64,576]{1,0:T(8,128)S(1)}, f32[64,576]{1,0:T(8,128)S(1)}, u32[]{:S(2)}, u32[]{:S(2)}) collective-permute-start(f32[64,576]{1,0:T(8,128)S(1)} %pad_maximum_fusion.refs_0_), channel_id=1, source_target_pairs={{0,16},{8,24},{1,17},{9,25},{2,18},{10,26},{3,19},{11,27},{4,20},{... | collective-permute-start | bytes 442376 | tf_op jit(solution)/shard_map/ppermute | solution.py:258
  22.9 6.2 %collective-permute-start.12 = (f32[64,576]{1,0:T(8,128)S(1)}, f32[64,576]{1,0:T(8,128)}, u32[]{:S(2)}, u32[]{:S(2)}) collective-permute-start(f32[64,576]{1,0:T(8,128)S(1)} %pad_maximum_fusion.refs_0_), channel_id=1, source_target_pairs={{0,24},{8,16},{1,25},{9,17},{2,26},{10,18},{3,27},{11,19},{4,28},{... | collective-permute-start | bytes 442376 | tf_op jit(solution)/shard_map/ppermute | solution.py:258
  24.9 6.6 %collective-permute-start.2 = (f32[16,2304]{1,0:T(8,128)}, f32[16,2304]{1,0:T(8,128)S(1)}, u32[]{:S(2)}, u32[]{:S(2)}) collective-permute-start(f32[16,2304]{1,0:T(8,128)} %refs_0_.1), channel_id=1, source_target_pairs={{0,6},{1,7},{2,0},{3,1},{4,2},{5,3},{6,4},{7,5},{8,14},{9,15},{10,... | collective-permute-start | bytes 442376 | tf_op jit(solution)/shard_map/ppermute | solution.py:252
  28.5 3.0 %collective-permute-start.13 = (f32[64,576]{1,0:T(8,128)S(1)}, f32[64,576]{1,0:T(8,128)}, u32[]{:S(2)}, u32[]{:S(2)}) collective-permute-start(f32[64,576]{1,0:T(8,128)S(1)} %pad_maximum_fusion.refs_0_), channel_id=1, source_target_pairs={{0,1},{1,0},{2,3},{3,2},{4,5},{5,4},{6,7},{7,6},{8,9},{9,8},{10,11... | collective-permute-start | bytes 442376 | tf_op jit(solution)/shard_map/ppermute | solution.py:247
  28.5 3.5 %collective-permute-start.14 = (f32[64,576]{1,0:T(8,128)S(1)}, f32[64,576]{1,0:T(8,128)}, u32[]{:S(2)}, u32[]{:S(2)}) collective-permute-start(f32[64,576]{1,0:T(8,128)S(1)} %collective-permute-done.10.refs_1_), channel_id=1, source_target_pairs={{0,1},{1,0},{2,3},{3,2},{4,5},{5,4},{6,7},{7,6},{8,9},{9,8},{10,11... | collective-permute-start | bytes 442376 | tf_op jit(solution)/shard_map/ppermute | solution.py:247
  29.0 3.1 %collective-permute-start.15 = (f32[64,576]{1,0:T(8,128)S(1)}, f32[64,576]{1,0:T(8,128)}, u32[]{:S(2)}, u32[]{:S(2)}) collective-permute-start(f32[64,576]{1,0:T(8,128)S(1)} %collective-permute-done.11.refs_2_), channel_id=1, source_target_pairs={{0,1},{1,0},{2,3},{3,2},{4,5},{5,4},{6,7},{7,6},{8,9},{9,8},{10,11... | collective-permute-start | bytes 442376 | tf_op jit(solution)/shard_map/ppermute | solution.py:247
  29.1 3.4 %collective-permute-start.16 = (f32[64,576]{1,0:T(8,128)}, f32[64,576]{1,0:T(8,128)}, u32[]{:S(2)}, u32[]{:S(2)}) collective-permute-start(f32[64,576]{1,0:T(8,128)} %collective-permute-done.12.refs_3_), channel_id=1, source_target_pairs={{0,1},{1,0},{2,3},{3,2},{4,5},{5,4},{6,7},{7,6},{8,9},{9,8},{10,11... | collective-permute-start | bytes 442376 | tf_op jit(solution)/shard_map/ppermute | solution.py:247
  31.5 5.2 %collective-permute-start.3 = (f32[16,2304]{1,0:T(8,128)}, f32[16,2304]{1,0:T(8,128)S(1)}, u32[]{:S(2)}, u32[]{:S(2)}) collective-permute-start(f32[16,2304]{1,0:T(8,128)} %refs_0_.1), channel_id=1, source_target_pairs={{0,1},{1,0},{2,3},{3,2},{4,5},{5,4},{6,7},{7,6},{8,9},{9,8},{10,11... | collective-permute-start | bytes 442376 | tf_op jit(solution)/shard_map/ppermute | solution.py:247
  31.5 5.3 %collective-permute-start.4 = (f32[16,2304]{1,0:T(8,128)S(1)}, f32[16,2304]{1,0:T(8,128)S(1)}, u32[]{:S(2)}, u32[]{:S(2)}) collective-permute-start(f32[16,2304]{1,0:T(8,128)S(1)} %collective-permute-done.refs_1_), channel_id=1, source_target_pairs={{0,1},{1,0},{2,3},{3,2},{4,5},{5,4},{6,7},{7,6},{8,9},{9,8},{10,11... | collective-permute-start | bytes 442376 | tf_op jit(solution)/shard_map/ppermute | solution.py:247
  32.0 4.8 %collective-permute-start.5 = (f32[16,2304]{1,0:T(8,128)S(1)}, f32[16,2304]{1,0:T(8,128)S(1)}, u32[]{:S(2)}, u32[]{:S(2)}) collective-permute-start(f32[16,2304]{1,0:T(8,128)S(1)} %collective-permute-done.1.refs_2_), channel_id=1, source_target_pairs={{0,1},{1,0},{2,3},{3,2},{4,5},{5,4},{6,7},{7,6},{8,9},{9,8},{10,11... | collective-permute-start | bytes 442376 | tf_op jit(solution)/shard_map/ppermute | solution.py:247
  32.1 4.7 %collective-permute-start.6 = (f32[16,2304]{1,0:T(8,128)S(1)}, f32[16,2304]{1,0:T(8,128)S(1)}, u32[]{:S(2)}, u32[]{:S(2)}) collective-permute-start(f32[16,2304]{1,0:T(8,128)S(1)} %collective-permute-done.2.refs_3_), channel_id=1, source_target_pairs={{0,1},{1,0},{2,3},{3,2},{4,5},{5,4},{6,7},{7,6},{8,9},{9,8},{10,11... | collective-permute-start | bytes 442376 | tf_op jit(solution)/shard_map/ppermute | solution.py:247
  47.6 2.1 %collective-permute-start.17 = (f32[64,2304]{1,0:T(8,128)S(1)}, f32[64,2304]{1,0:T(8,128)S(1)}, u32[]{:S(2)}, u32[]{:S(2)}) collective-permute-start(f32[64,2304]{1,0:T(8,128)S(1)} %get-tuple-element.16), channel_id=1, source_target_pairs={{0,1},{1,0},{2,3},{3,2},{4,5},{5,4},{6,7},{7,6},{8,9},{9,8},{10,11... | collective-permute-start | bytes 1769480 | tf_op jit(solution)/shard_map/ppermute | solution.py:247
  49.8 9.0 %collective-permute-start.18 = (f32[16,2304]{1,0:T(8,128)S(1)}, f32[16,2304]{1,0:T(8,128)S(1)}, u32[]{:S(2)}, u32[]{:S(2)}) collective-permute-start(f32[16,2304]{1,0:T(8,128)S(1)} %get-tuple-element.20), channel_id=1, source_target_pairs={{0,2},{1,3},{2,4},{3,5},{4,6},{5,7},{6,0},{7,1},{8,10},{9,11},{10,... | collective-permute-start | bytes 442376 | tf_op jit(solution)/shard_map/ppermute | solution.py:252
  50.7 13.9 %collective-permute-start.19 = (f32[16,2304]{1,0:T(8,128)S(1)}, f32[16,2304]{1,0:T(8,128)S(1)}, u32[]{:S(2)}, u32[]{:S(2)}) collective-permute-start(f32[16,2304]{1,0:T(8,128)S(1)} %get-tuple-element.22), channel_id=1, source_target_pairs={{0,4},{1,5},{2,6},{3,7},{4,0},{5,1},{6,2},{7,3},{8,12},{9,13},{10,... | collective-permute-start | bytes 442376 | tf_op jit(solution)/shard_map/ppermute | solution.py:252
  54.6 10.0 %collective-permute-start.20 = (f32[16,2304]{1,0:T(8,128)S(1)}, f32[16,2304]{1,0:T(8,128)S(1)}, u32[]{:S(2)}, u32[]{:S(2)}) collective-permute-start(f32[16,2304]{1,0:T(8,128)S(1)} %get-tuple-element.21), channel_id=1, source_target_pairs={{0,6},{1,7},{2,0},{3,1},{4,2},{5,3},{6,4},{7,5},{8,14},{9,15},{10,... | collective-permute-start | bytes 442376 | tf_op jit(solution)/shard_map/ppermute | solution.py:252
  (3 other events, 10.9 us)
